TPU v7x, 32 devices: a whole 2x2x4 slice. The times are simulated.
32 devices in a mesh: groups: 2 (over y), cells: 4 (over z), nodes: 2 (over x), sub: 2 (over core).
Axes of the slice: x: 2, y: 2, z: 4, core: 2. Of those that a mesh axis runs over, the one named last changes fastest.
Arguments:
- adjoint_start: float32 [4, 5, 16384], P('nodes', None, ('groups', 'cells', 'sub')), parts along dimension 2, may hold values from -6 to 6
- adjoint_rhs: float32 [4, 5, 16384], P('nodes', None, ('groups', 'cells', 'sub')), parts along dimension 2, may hold values from -6 to 6
- off_blocks: bfloat16 [4, 6, 25, 16384], P('nodes', None, None, ('groups', 'cells', 'sub')), parts along dimension 3, may hold values from -0.5 to 0.5
- diag_inverse: float32 [4, 25, 16384], P('nodes', None, ('groups', 'cells', 'sub')), parts along dimension 2, may hold values from -2.4 to 2.4
- neighbours: int32 [6, 8192], P(None, ('cells', 'sub')), may hold values from -1 to 8191, as said below
- node_weights: float32 [4], P('nodes'), may hold values from 0.05 to 0.5
- sens_blocks: bfloat16 [4, 15, 16384], P('nodes', None, ('groups', 'cells', 'sub')), parts along dimension 2, may hold values from -1.796875 to 1.796875
- cell_points: float32 [3, 8192], P(None, ('cells', 'sub')), may hold values from 0 to 1
- base_points: float32 [3, 4096], replicated, may hold values from 0 to 1
- ffd_index: int32 [4096, 8], replicated, may hold values from 0 to 511
- ffd_weight: float32 [4096, 8], replicated, may hold values from 0 to 1
Outputs:
- adjoint: float32 [4, 5, 16384], P('nodes', None, ('groups', 'cells', 'sub')), parts along dimension 2
- control_grad: float32 [6, 512], P('groups'), parts along dimension 0
There are 2 independent parts, one for each index of `groups`. A program takes and returns all parts, laid end to end along the dimension named above; an argument that names none is the same for every part. Nothing has to cross between parts.
Inputs may be any that keep to these rules, and one draw needn't show every extreme that they name: `neighbours`: each entry is -1 (no neighbour) or the index of a cell at most 1024 away from the cell; the distance 1024 occurs.
All inputs are finite; a program needn't handle non-finite values.
Results may differ from a plain program's by a relative error of at most 0.0003.
Values sent between devices are 32-bit elements; how exact they have to be, the bound alone decides.
A program may use at most 64 MiB of HBM per device.

v0:
```python
import jax
import jax.numpy as jnp
from jax import lax
from jax.sharding import PartitionSpec as P

SWEEPS = 2
FFD = 512


support_radius = 0.3


def with_halo(array, sides, width):
    for axis, dim in sides:
        peers, length = (lax.axis_size(axis), array.shape[dim])
        up = [(i, (i + 1) % peers) for i in range(peers - 1)]
        down = [(j, i) for i, j in up]
        last = lax.slice_in_dim(array, length - width, length, axis=dim)
        initial = lax.slice_in_dim(array, 0, width, axis=dim)
        before = lax.ppermute(last, axis, up)
        after = lax.ppermute(initial, axis, down)
        array = jnp.concatenate([before, array, after], axis=dim)
    return array


def relax(adjoint, adjoint_rhs, off_blocks, diag_inverse, present, local_index):
    cell_count = adjoint.shape[2]
    node_count = adjoint.shape[0]
    widened = with_halo(adjoint, ((("cells", "sub"), 2),), cell_count)
    coupled = jnp.zeros(adjoint.shape, jnp.float32)
    for face_slot in range(off_blocks.shape[1]):
        beside = jnp.where(
            present[face_slot][None, None, :], widened[:, :, local_index[face_slot]], 0.0
        )
        coupling = (
            off_blocks[:, face_slot].astype(jnp.float32).reshape(node_count, 5, 5, cell_count)
        )
        coupled = coupled + jnp.sum(coupling * beside[:, None], axis=2)
    inverse = diag_inverse.reshape(node_count, 5, 5, cell_count)
    return jnp.sum(inverse * (adjoint_rhs - coupled)[:, None], axis=2)


def kernel_sum(sensitivity, points, base):
    squared = jnp.zeros((points.shape[1], base.shape[1]), jnp.float32)
    for axis_slot in range(3):
        squared = squared + (points[axis_slot][:, None] - base[axis_slot][None, :]) ** 2
    ratio = jnp.sqrt(squared) / support_radius
    kernel = jnp.maximum(1.0 - ratio, 0.0) ** 4 * (4.0 * ratio + 1.0)
    return jnp.dot(
        sensitivity, kernel, precision=lax.Precision.HIGHEST, preferred_element_type=jnp.float32
    )


def lattice_matrix(lattice_index, lattice_weight, columns):
    matches = lattice_index[:, :, None] == jnp.arange(columns, dtype=jnp.int32)[None, None, :]
    return jnp.sum(jnp.where(matches, lattice_weight[:, :, None], 0.0), axis=1)


def body(
    adjoint_start,
    adjoint_rhs,
    off_blocks,
    diag_inverse,
    neighbours,
    node_weights,
    sens_blocks,
    cell_points,
    base_points,
    ffd_index,
    ffd_weight,
):
    cell_count = adjoint_start.shape[2]
    first_cell = lax.axis_index(("cells", "sub")) * cell_count
    present = neighbours >= 0
    local_index = jnp.where(present, neighbours - first_cell + cell_count, 0)
    adjoint = adjoint_start
    for sweep_step in range(SWEEPS):
        adjoint = relax(adjoint, adjoint_rhs, off_blocks, diag_inverse, present, local_index)
    node_count = adjoint.shape[0]
    derive = sens_blocks.astype(jnp.float32).reshape(node_count, 5, 3, cell_count)
    per_node = jnp.sum(adjoint[:, :, None] * derive, axis=1)
    partial_sens = jnp.sum(node_weights[:, None, None] * per_node, axis=0)
    share_count = cell_count // lax.axis_size("nodes")
    share_start = lax.axis_index("nodes") * share_count
    node_sum = lax.psum(partial_sens, "nodes")
    sensitivity = lax.dynamic_slice_in_dim(node_sum, share_start, share_count, 1)
    points = lax.dynamic_slice_in_dim(cell_points, share_start, share_count, 1)
    base_count = base_points.shape[1]
    base_block = min(512, base_count)
    pieces = []
    for block_index in range(base_count // base_block):
        base_part = base_points[:, block_index * base_block : (block_index + 1) * base_block]
        pieces.append(kernel_sum(sensitivity, points, base_part))
    g_part = jnp.concatenate(pieces, axis=1)
    scale = 1.0 / jnp.sqrt(jnp.float32(cell_count * lax.axis_size(("cells", "sub"))))
    columns = FFD
    owned = base_count // lax.axis_size(("cells", "nodes", "sub"))
    owner_start = lax.axis_index(("cells", "nodes", "sub")) * owned
    base_grad = (
        lax.psum_scatter(g_part, ("cells", "nodes", "sub"), scatter_dimension=1, tiled=True) * scale
    )
    lattice_index = lax.dynamic_slice_in_dim(ffd_index, owner_start, owned, 0)
    lattice_weight = lax.dynamic_slice_in_dim(ffd_weight, owner_start, owned, 0)
    lattice = lattice_matrix(lattice_index, lattice_weight, columns)
    own_grad = jnp.dot(
        base_grad, lattice, precision=lax.Precision.HIGHEST, preferred_element_type=jnp.float32
    )
    control_grad = lax.psum(own_grad, ("cells", "nodes", "sub"))
    return (adjoint, control_grad)


def solution(mesh):
    return jax.shard_map(
        body,
        mesh=mesh,
        in_specs=(
            P("nodes", None, ("groups", "cells", "sub")),
            P("nodes", None, ("groups", "cells", "sub")),
            P("nodes", None, None, ("groups", "cells", "sub")),
            P("nodes", None, ("groups", "cells", "sub")),
            P(None, ("cells", "sub")),
            P("nodes"),
            P("nodes", None, ("groups", "cells", "sub")),
            P(None, ("cells", "sub")),
            P(),
            P(),
            P(),
        ),
        out_specs=(P("nodes", None, ("groups", "cells", "sub")), P("groups", None)),
        check_vma=False,
    )
```

profile of v0, /device:TPU:0, one launch (start us, length us, event | category | flops | bytes accessed | tf_op | source)
XLA Modules:
  0.0 309.3 jit_solution(3301898094393572463)
XLA Ops:
  20.1 3.8 %copy.58 = f32[2,5,3072]{1,0,2:T(2,128)S(1)} copy(f32[2,5,3072]{2,0,1:T(2,128)} %pad_maximum_fusion) | data formatting | bytes 245760 | tf_op jit(solution)/shard_map/concatenate | solution.py:22
  24.0 7.7 %gather_fusion = f32[1024,2,5]{2,1,0:T(2,128)} fusion(f32[2,5,3072]{1,0,2:T(2,128)S(1)} %copy.58, s32[1024]{0:T(1024)S(1)} %get-tuple-element.52), kind=kCustom, calls=%fused_computation | custom fusion | bytes 86016 | tf_op jit(solution)/shard_map/gather | solution.py:33
  31.7 5.3 %select_bitcast_fusion.11 = f32[2,5,1024]{1,0,2:T(2,128)S(1)} fusion(f32[1024,2,5]{2,1,0:T(2,128)} %gather_fusion, pred[1024]{0:T(1024)(128)(4,1)S(1)} %get-tuple-element.7), kind=kLoop, calls=%fused_computation.33 | loop fusion | flops 10240 | bytes 82944 | tf_op jit(solution)/shard_map/jit(_where)/select_n | solution.py:32
  37.4 5.4 %gather_fusion.1 = f32[1024,2,5]{2,1,0:T(2,128)S(1)} fusion(f32[2,5,3072]{1,0,2:T(2,128)} %copy-done.1, s32[1024]{0:T(1024)S(1)} %get-tuple-element.51), kind=kCustom, calls=%fused_computation.1 | custom fusion | bytes 86016 | tf_op jit(solution)/shard_map/gather | solution.py:33
  42.9 3.7 %select_bitcast_fusion.10 = f32[2,5,1024]{1,0,2:T(2,128)S(1)} fusion(f32[1024,2,5]{2,1,0:T(2,128)S(1)} %gather_fusion.1, pred[1024]{0:T(1024)(128)(4,1)S(1)} %get-tuple-element.2), kind=kLoop, calls=%fused_computation.32 | loop fusion | flops 10240 | bytes 82944 | tf_op jit(solution)/shard_map/jit(_where)/select_n | solution.py:32
  47.1 5.4 %gather_fusion.2 = f32[1024,2,5]{2,1,0:T(2,128)S(1)} fusion(f32[2,5,3072]{1,0,2:T(2,128)} %copy-done.1, s32[1024]{0:T(1024)S(1)} %get-tuple-element.50), kind=kCustom, calls=%fused_computation.2 | custom fusion | bytes 86016 | tf_op jit(solution)/shard_map/gather | solution.py:33
  56.8 5.4 %gather_fusion.3 = f32[1024,2,5]{2,1,0:T(2,128)S(1)} fusion(f32[2,5,3072]{1,0,2:T(2,128)} %copy-done.1, s32[1024]{0:T(1024)S(1)} %get-tuple-element.49), kind=kCustom, calls=%fused_computation.3 | custom fusion | bytes 86016 | tf_op jit(solution)/shard_map/gather | solution.py:33
  66.4 5.4 %gather_fusion.4 = f32[1024,2,5]{2,1,0:T(2,128)S(1)} fusion(f32[2,5,3072]{1,0,2:T(2,128)} %copy-done.1, s32[1024]{0:T(1024)S(1)} %get-tuple-element.48), kind=kCustom, calls=%fused_computation.4 | custom fusion | bytes 86016 | tf_op jit(solution)/shard_map/gather | solution.py:33
  76.1 5.4 %gather_fusion.5 = f32[1024,2,5]{2,1,0:T(2,128)S(1)} fusion(f32[2,5,3072]{1,0,2:T(2,128)} %copy-done.1, s32[1024]{0:T(1024)S(1)} %get-tuple-element.47), kind=kCustom, calls=%fused_computation.5 | custom fusion | bytes 86016 | tf_op jit(solution)/shard_map/gather | solution.py:33
  81.6 3.7 %select_bitcast_fusion.6 = f32[2,5,1024]{1,0,2:T(2,128)S(1)} fusion(f32[1024,2,5]{2,1,0:T(2,128)S(1)} %gather_fusion.5, pred[1024]{0:T(1024)(128)(4,1)S(1)} %get-tuple-element.6), kind=kLoop, calls=%fused_computation.28 | loop fusion | flops 10240 | bytes 82944 | tf_op jit(solution)/shard_map/jit(_where)/select_n | solution.py:32
  86.8 5.2 %collective-permute-start.2 = (f32[2,5,1024]{2,0,1:T(2,128)S(1)}, f32[2,5,1024]{2,0,1:T(2,128)S(1)}, u32[]{:S(2)}, u32[]{:S(2)}) collective-permute-start(f32[2,5,1024]{2,0,1:T(2,128)S(1)} %multiply_reduce_fusion.1), channel_id=1, source_target_pairs={{0,1},{1,4},{4,5},{5,8},{8,9},{9,12},{12,13},{2,3},{3,6},{6,7},{7,... | collective-permute-start | bytes 122888 | tf_op jit(solution)/shard_map/ppermute | solution.py:20
  97.3 3.8 %copy.70 = f32[2,5,3072]{1,0,2:T(2,128)S(1)} copy(f32[2,5,3072]{2,0,1:T(2,128)} %pad_maximum_fusion.1) | data formatting | bytes 245760 | tf_op jit(solution)/shard_map/concatenate | solution.py:22
  101.1 7.5 %gather_fusion.6 = f32[1024,2,5]{2,1,0:T(2,128)} fusion(f32[2,5,3072]{1,0,2:T(2,128)S(1)} %copy.70, s32[1024]{0:T(1024)S(1)} %get-tuple-element.52), kind=kCustom, calls=%fused_computation.6 | custom fusion | bytes 86016 | tf_op jit(solution)/shard_map/gather | solution.py:33
  108.6 7.5 %gather_fusion.7 = f32[1024,2,5]{2,1,0:T(2,128)} fusion(f32[2,5,3072]{1,0,2:T(2,128)S(1)} %copy.70, s32[1024]{0:T(1024)S(1)} %get-tuple-element.51), kind=kCustom, calls=%fused_computation.7 | custom fusion | bytes 86016 | tf_op jit(solution)/shard_map/gather | solution.py:33
  116.0 7.4 %gather_fusion.8 = f32[1024,2,5]{2,1,0:T(2,128)} fusion(f32[2,5,3072]{1,0,2:T(2,128)S(1)} %copy.70, s32[1024]{0:T(1024)S(1)} %get-tuple-element.50), kind=kCustom, calls=%fused_computation.8 | custom fusion | bytes 86016 | tf_op jit(solution)/shard_map/gather | solution.py:33
  123.5 7.5 %gather_fusion.9 = f32[1024,2,5]{2,1,0:T(2,128)} fusion(f32[2,5,3072]{1,0,2:T(2,128)S(1)} %copy.70, s32[1024]{0:T(1024)S(1)} %get-tuple-element.49), kind=kCustom, calls=%fused_computation.9 | custom fusion | bytes 86016 | tf_op jit(solution)/shard_map/gather | solution.py:33
  130.9 7.5 %gather_fusion.10 = f32[1024,2,5]{2,1,0:T(2,128)} fusion(f32[2,5,3072]{1,0,2:T(2,128)S(1)} %copy.70, s32[1024]{0:T(1024)S(1)} %get-tuple-element.48), kind=kCustom, calls=%fused_computation.10 | custom fusion | bytes 86016 | tf_op jit(solution)/shard_map/gather | solution.py:33
  138.4 7.5 %gather_fusion.11 = f32[1024,2,5]{2,1,0:T(2,128)} fusion(f32[2,5,3072]{1,0,2:T(2,128)S(1)} %copy.70, s32[1024]{0:T(1024)S(1)} %get-tuple-element.47), kind=kCustom, calls=%fused_computation.11 | custom fusion | bytes 86016 | tf_op jit(solution)/shard_map/gather | solution.py:33
  145.9 5.4 %select_bitcast_fusion.5 = f32[2,5,1024]{1,0,2:T(2,128)S(1)} fusion(f32[1024,2,5]{2,1,0:T(2,128)} %gather_fusion.6, pred[1024]{0:T(1024)(128)(4,1)S(1)} %get-tuple-element.7), kind=kLoop, calls=%fused_computation.27 | loop fusion | flops 10240 | bytes 82944 | tf_op jit(solution)/shard_map/jit(_where)/select_n | solution.py:32
  165.2 5.4 %select_bitcast_fusion.2 = f32[2,5,1024]{1,0,2:T(2,128)S(1)} fusion(f32[1024,2,5]{2,1,0:T(2,128)} %gather_fusion.9, pred[1024]{0:T(1024)(128)(4,1)S(1)} %get-tuple-element.4), kind=kLoop, calls=%fused_computation.24 | loop fusion | flops 10240 | bytes 82944 | tf_op jit(solution)/shard_map/jit(_where)/select_n | solution.py:32
  177.1 3.7 %select_bitcast_fusion = f32[2,5,1024]{1,0,2:T(2,128)S(1)} fusion(f32[1024,2,5]{2,1,0:T(2,128)S(1)} %copy-done.2, pred[1024]{0:T(1024)(128)(4,1)S(1)} %get-tuple-element.6), kind=kLoop, calls=%fused_computation.22 | loop fusion | flops 10240 | bytes 82944 | tf_op jit(solution)/shard_map/jit(_where)/select_n | solution.py:32
  183.7 8.1 %psum.14 = f32[3,1024]{1,0:T(4,128)S(1)} all-reduce(f32[3,1024]{1,0:T(4,128)S(1)} %multiply_reduce_fusion.2), channel_id=1, replica_groups=mesh['groups'=2,'cells'=4,'nodes'=2,'sub'=2] {'nodes'}, use_global_device_ids=true, to_apply=%region_16.17 | all-reduce | flops 3072 | bytes 24576 | tf_op jit(solution)/shard_map/psum | solution.py:85
  207.4 63.1 %reduce-scatter.4.cloned.1.call-done = f32[256,3]{1,0:T(8,128)} async-done(((f32[4096,3]{1,0:T(8,128)}), f32[256,3]{1,0:T(8,128)}) %reduce-scatter.4.cloned.1.call-update) | async-done | bytes 3088
  271.9 30.6 %psum.15 = f32[3,512]{1,0:T(4,128)} all-reduce(f32[3,512]{1,0:T(4,128)S(1)} %fusion.229), channel_id=1, replica_groups=mesh['groups'=2,'cells'=4,'nodes'=2,'sub'=2] {'cells','nodes','sub'}, use_global_device_ids=true, to_apply=%region_19.20 | all-reduce | flops 1536 | bytes 12288 | tf_op jit(solution)/shard_map/psum | solution.py:108
  (162 shorter events, 72.8 us)
Async XLA Ops:
  7.2 263.3 %reduce-scatter.4.cloned.1.call-start = ((), (), s32[]{:S(2)}) async-start(), calls=%async_computation.1 | async-start | bytes 2228224
  7.2 11.4 %collective-permute-start = (f32[2,5,1024]{2,0,1:T(2,128)}, f32[2,5,1024]{2,0,1:T(2,128)S(1)}, u32[]{:S(2)}, u32[]{:S(2)}) collective-permute-start(f32[2,5,1024]{2,0,1:T(2,128)} %param.11), channel_id=1, source_target_pairs={{0,1},{1,4},{4,5},{5,8},{8,9},{9,12},{12,13},{2,3},{3,6},{6,7},{7,... | collective-permute-start | bytes 122888 | tf_op jit(solution)/shard_map/ppermute | solution.py:20
  9.6 9.0 %collective-permute-start.1 = (f32[2,5,1024]{2,0,1:T(2,128)}, f32[2,5,1024]{2,0,1:T(2,128)S(1)}, u32[]{:S(2)}, u32[]{:S(2)}) collective-permute-start(f32[2,5,1024]{2,0,1:T(2,128)} %param.11), channel_id=1, source_target_pairs={{1,0},{4,1},{5,4},{8,5},{9,8},{12,9},{13,12},{3,2},{6,3},{7,6},{10... | collective-permute-start | bytes 122888 | tf_op jit(solution)/shard_map/ppermute | solution.py:21
  71.9 13.9 %copy-start.9 = (bf16[2,1,25,1024]{3,0,2,1:T(2,128)(2,1)S(1)}, bf16[2,1,25,1024]{3,0,2,1:T(2,128)(2,1)}, u32[]{:S(2)}) copy-start(bf16[2,1,25,1024]{3,0,2,1:T(2,128)(2,1)} %get-tuple-element.11) | copy-start | bytes 307204
  71.9 14.1 %copy-start.8 = (bf16[2,1,25,1024]{3,0,2,1:T(2,128)(2,1)S(1)}, bf16[2,1,25,1024]{3,0,2,1:T(2,128)(2,1)}, u32[]{:S(2)}) copy-start(bf16[2,1,25,1024]{3,0,2,1:T(2,128)(2,1)} %get-tuple-element.8) | copy-start | bytes 307204
  71.9 14.2 %copy-start.7 = (bf16[2,1,25,1024]{3,0,2,1:T(2,128)(2,1)S(1)}, bf16[2,1,25,1024]{3,0,2,1:T(2,128)(2,1)}, u32[]{:S(2)}) copy-start(bf16[2,1,25,1024]{3,0,2,1:T(2,128)(2,1)} %get-tuple-element.10) | copy-start | bytes 307204
  71.9 14.3 %copy-start.6 = (bf16[2,1,25,1024]{3,0,2,1:T(2,128)(2,1)S(1)}, bf16[2,1,25,1024]{3,0,2,1:T(2,128)(2,1)}, u32[]{:S(2)}) copy-start(bf16[2,1,25,1024]{3,0,2,1:T(2,128)(2,1)} %get-tuple-element.9) | copy-start | bytes 307204
  75.7 10.9 %copy-start.13 = (f32[2,5,1024]{2,0,1:T(2,128)S(1)}, f32[2,5,1024]{2,0,1:T(2,128)}, u32[]{:S(2)}) copy-start(f32[2,5,1024]{2,0,1:T(2,128)} %param.12) | copy-start | bytes 122884
  75.7 11.0 %copy-start.10 = (f32[2,25,1024]{2,0,1:T(2,128)S(1)}, f32[2,25,1024]{2,0,1:T(2,128)}, u32[]{:S(2)}) copy-start(f32[2,25,1024]{2,0,1:T(2,128)} %param.14) | copy-start | bytes 614404
  86.8 9.8 %collective-permute-start.2 = (f32[2,5,1024]{2,0,1:T(2,128)S(1)}, f32[2,5,1024]{2,0,1:T(2,128)S(1)}, u32[]{:S(2)}, u32[]{:S(2)}) collective-permute-start(f32[2,5,1024]{2,0,1:T(2,128)S(1)} %multiply_reduce_fusion.1), channel_id=1, source_target_pairs={{0,1},{1,4},{4,5},{5,8},{8,9},{9,12},{12,13},{2,3},{3,6},{6,7},{7,... | collective-permute-start | bytes 122888 | tf_op jit(solution)/shard_map/ppermute | solution.py:20
  92.0 4.5 %collective-permute-start.3 = (f32[2,5,1024]{2,0,1:T(2,128)S(1)}, f32[2,5,1024]{2,0,1:T(2,128)S(1)}, u32[]{:S(2)}, u32[]{:S(2)}) collective-permute-start(f32[2,5,1024]{2,0,1:T(2,128)S(1)} %multiply_reduce_fusion.1), channel_id=1, source_target_pairs={{1,0},{4,1},{5,4},{8,5},{9,8},{12,9},{13,12},{3,2},{6,3},{7,6},{10... | collective-permute-start | bytes 122888 | tf_op jit(solution)/shard_map/ppermute | solution.py:21
  145.9 13.4 %copy-start.4 = (f32[1024,2,5]{2,1,0:T(2,128)S(1)}, f32[1024,2,5]{2,1,0:T(2,128)}, u32[]{:S(2)}) copy-start(f32[1024,2,5]{2,1,0:T(2,128)} %gather_fusion.8) | copy-start | bytes 122884
  159.3 13.4 %copy-start.3 = (f32[1024,2,5]{2,1,0:T(2,128)S(1)}, f32[1024,2,5]{2,1,0:T(2,128)}, u32[]{:S(2)}) copy-start(f32[1024,2,5]{2,1,0:T(2,128)} %gather_fusion.10) | copy-start | bytes 122884
  165.2 11.9 %copy-start.2 = (f32[1024,2,5]{2,1,0:T(2,128)S(1)}, f32[1024,2,5]{2,1,0:T(2,128)}, u32[]{:S(2)}) copy-start(f32[1024,2,5]{2,1,0:T(2,128)} %gather_fusion.11) | copy-start | bytes 122884
  176.4 15.4 %copy-start.31 = (f32[1,512]{1,0:T(1,128)S(1)}, f32[1,512]{1,0:T(1,128)}, u32[]{:S(2)}) copy-start(f32[1,512]{1,0:T(1,128)} %get-tuple-element.34) | copy-start | bytes 6148
  176.4 15.4 %copy-start.32 = (f32[1,512]{1,0:T(1,128)S(1)}, f32[1,512]{1,0:T(1,128)}, u32[]{:S(2)}) copy-start(f32[1,512]{1,0:T(1,128)} %get-tuple-element.35) | copy-start | bytes 6148
  176.4 15.4 %copy-start.33 = (f32[1,512]{1,0:T(1,128)S(1)}, f32[1,512]{1,0:T(1,128)}, u32[]{:S(2)}) copy-start(f32[1,512]{1,0:T(1,128)} %get-tuple-element.36) | copy-start | bytes 6148
  176.4 15.4 %copy-start.40 = (f32[1,512]{1,0:T(1,128)S(1)}, f32[1,512]{1,0:T(1,128)}, u32[]{:S(2)}) copy-start(f32[1,512]{1,0:T(1,128)} %get-tuple-element.44) | copy-start | bytes 6148
  176.9 14.9 %copy-start.41 = (f32[1,512]{1,0:T(1,128)S(1)}, f32[1,512]{1,0:T(1,128)}, u32[]{:S(2)}) copy-start(f32[1,512]{1,0:T(1,128)} %get-tuple-element.45) | copy-start | bytes 6148
  176.9 14.9 %copy-start.42 = (f32[1,512]{1,0:T(1,128)S(1)}, f32[1,512]{1,0:T(1,128)}, u32[]{:S(2)}) copy-start(f32[1,512]{1,0:T(1,128)} %get-tuple-element.46) | copy-start | bytes 6148
  180.8 12.5 %copy-start.37 = (f32[1,512]{1,0:T(1,128)S(1)}, f32[1,512]{1,0:T(1,128)}, u32[]{:S(2)}) copy-start(f32[1,512]{1,0:T(1,128)} %get-tuple-element.30) | copy-start | bytes 6148
  180.9 12.5 %copy-start.38 = (f32[1,512]{1,0:T(1,128)S(1)}, f32[1,512]{1,0:T(1,128)}, u32[]{:S(2)}) copy-start(f32[1,512]{1,0:T(1,128)} %get-tuple-element.31) | copy-start | bytes 6148
  180.9 12.5 %copy-start.39 = (f32[1,512]{1,0:T(1,128)S(1)}, f32[1,512]{1,0:T(1,128)}, u32[]{:S(2)}) copy-start(f32[1,512]{1,0:T(1,128)} %get-tuple-element.32) | copy-start | bytes 6148
  183.4 11.3 %copy-start.15 = (f32[2,5,1024]{2,0,1:T(2,128)}, f32[2,5,1024]{2,0,1:T(2,128)S(1)}, u32[]{:S(2)}) copy-start(f32[2,5,1024]{2,0,1:T(2,128)S(1)} %multiply_reduce_fusion) | copy-start | bytes 122884
  (25 other events, 80.9 us)
Sparse Core Ops, SparseCore 0:
  205.8 64.6 reduce-scatter.3
where the time goes:
time: 311 us; the launch traced here: 309 us
  local copies, waits for them, and re-layouts  105 us (34%)
  other arithmetic  65 us (21%)
  waiting for transfers between devices  63.1 us (20%)
  blocking collectives  38.8 us (12%)
  between operations  14.8 us (5%)
  matrix products  11.9 us (4%)
  starting transfers between devices  10.4 us (3%)
    gather x12, local copies, waits for them, and re-layouts, relax(): widened[:, :, local_index[face_slot]]  79.7 us
    unnamed x2, waiting for transfers between devices  63.1 us
    select_n x12, other arithmetic, relax(): jnp.where(present[face_slot][None, None, :], widened[:, :, local_index[fa...  49.7 us
    psum x1, blocking collectives, body(): control_grad = lax.psum(own_grad, ('cells', 'nodes', 'sub'))  30.6 us
    dot_general x8, matrix products, kernel_sum(): jnp.dot(sensitivity, kernel, precision=lax.Precision.HIGHEST, preferred_e...  11.6 us
    psum x1, blocking collectives, body(): node_sum = lax.psum(partial_sens, 'nodes')  8.15 us
    ppermute x2, starting transfers between devices, with_halo(): before = lax.ppermute(last, axis, up)  7.65 us
    reduce_sum x12, other arithmetic, relax(): coupled = coupled + jnp.sum(coupling * beside[:, None], axis=2)  7.63 us
  transfers between devices with their start and end apart: 5, of which 1 were waited for; matrix products, arithmetic and copies ran while one was open for 4% of the time, Pallas kernels for 0%

commit v1 on v0

v1 whole, which is shorter than its diff:
```python
import functools

import jax
import jax.numpy as jnp
from jax import lax
from jax.experimental import pallas as pl
from jax.experimental.pallas import tpu as pltpu
from jax.sharding import PartitionSpec as P

SWEEPS = 2
FFD = 512
LANES = 128
ROWS = 8
TILE = 256

support_radius = 0.3
MESH = pl.DeviceIdType.MESH


def split2(x):
    hi = x.astype(jnp.bfloat16)
    return hi, (x - hi.astype(jnp.float32)).astype(jnp.bfloat16)


def split3(x):
    one = x.astype(jnp.bfloat16).astype(jnp.float32)
    two = (x - one).astype(jnp.bfloat16).astype(jnp.float32)
    return one, two, (x - one) - two


def kernel(
    scale,
    weight_ref,
    adj_ref,
    rhs_ref,
    nb_ref,
    sens_ref,
    point_ref,
    base_ref,
    ffd_index_ref,
    ffd_weight_ref,
    off_hbm,
    inv_hbm,
    out_ref,
    grad_ref,
    off_ref,
    inv_ref,
    wide,
    win,
    rel_ref,
    lane_ref,
    points,
    cell_feat,
    base_feat,
    k_hi,
    k_lo,
    l_hi,
    l_lo,
    sens_rows,
    sens_slots,
    sens_mat,
    grad_slots,
    load_sem,
    halo_send,
    halo_recv,
    point_send,
    point_recv,
    sens_send,
    sens_recv,
    grad_send,
    grad_recv,
):
    cells, subs, nodes = (lax.axis_size(a) for a in ("cells", "sub", "nodes"))
    cell_at, sub_at, node_at = (lax.axis_index(a) for a in ("cells", "sub", "nodes"))
    here, places = cell_at * subs + sub_at, cells * subs
    team, crew = node_at * subs + sub_at, nodes * subs
    me, everyone = cell_at * crew + team, cells * crew
    nodes_here = weight_ref.shape[0]
    rows = adj_ref.shape[1]
    blocks = rows // nodes_here
    cell_count = blocks * LANES
    base_own = base_feat.shape[1]

    def member(index):
        return {"nodes": index // subs, "sub": index % subs}

    def anyone(index):
        return dict(member(index % crew), cells=index // crew)

    barrier = pltpu.get_barrier_semaphore()
    for step in range(1, everyone):
        pl.semaphore_signal(
            barrier, inc=1, device_id=anyone((me + step) % everyone), device_id_type=MESH
        )
    off_load = pltpu.make_async_copy(off_hbm, off_ref, load_sem.at[0])
    inv_load = pltpu.make_async_copy(inv_hbm, inv_ref, load_sem.at[1])
    off_load.start()
    inv_load.start()

    wide[0, :, rows : 2 * rows, :] = adj_ref[...]

    first_cell = here * cell_count
    for face in range(nb_ref.shape[0]):
        for block in range(blocks):
            entry = nb_ref[face : face + 1, block * LANES : (block + 1) * LANES]
            local = entry - first_cell + cell_count
            chunk = jnp.where(entry >= 0, (local >> 7) - block, -1)
            span = pl.ds(block * nodes_here, nodes_here)
            rel_ref[face, span, :] = jnp.broadcast_to(chunk, (nodes_here, LANES))
            lane_ref[face, span, :] = jnp.broadcast_to(local & (LANES - 1), (nodes_here, LANES))

    base_start = team * base_own

    def build_lattice(step, carry):
        source = pl.ds(pl.multiple_of(base_start + step * LANES, LANES), LANES)
        target = pl.ds(pl.multiple_of(step * LANES, LANES), LANES)
        index = ffd_index_ref[:, source]
        weight = ffd_weight_ref[:, source]
        group = 64
        row = lax.broadcasted_iota(jnp.int32, (group, LANES), 0)
        for top in range(0, FFD, group):
            total = jnp.zeros((group, LANES), jnp.float32)
            for slot in range(index.shape[0]):
                match = row == index[slot : slot + 1, :] - top
                total = total + jnp.where(match, weight[slot : slot + 1, :], 0.0)
            hi, lo = split2(total)
            l_hi[top : top + group, target] = hi
            l_lo[top : top + group, target] = lo
        return carry

    lax.fori_loop(0, base_own // LANES, build_lattice, 0)

    @pl.when(here == 0)
    def _():
        wide[:, :, 0:rows, :] = jnp.zeros((SWEEPS, 5, rows, LANES), jnp.float32)

    @pl.when(here == places - 1)
    def _():
        wide[:, :, 2 * rows : 3 * rows, :] = jnp.zeros((SWEEPS, 5, rows, LANES), jnp.float32)

    pl.semaphore_wait(barrier, everyone - 1)

    def halo(sweep, side):
        other = here + 1 if side == 0 else here - 1
        start = 0 if side == 0 else 2 * rows
        return pltpu.make_async_remote_copy(
            src_ref=wide.at[sweep, :, pl.ds(rows, rows), :],
            dst_ref=wide.at[sweep, :, pl.ds(start, rows), :],
            send_sem=halo_send.at[sweep, side],
            recv_sem=halo_recv.at[sweep, side],
            device_id={"cells": other // subs, "sub": other % subs},
            device_id_type=MESH,
        )

    def halo_start(sweep):
        @pl.when(here < places - 1)
        def _():
            halo(sweep, 0).start()

        @pl.when(here > 0)
        def _():
            halo(sweep, 1).start()

    def halo_wait(sweep):
        @pl.when(here > 0)
        def _():
            halo(sweep, 0).wait_recv()

        @pl.when(here < places - 1)
        def _():
            halo(sweep, 1).wait_recv()

    def halo_sent(sweep):
        @pl.when(here < places - 1)
        def _():
            halo(sweep, 0).wait_send()

        @pl.when(here > 0)
        def _():
            halo(sweep, 1).wait_send()

    def point_copy(step):
        return pltpu.make_async_remote_copy(
            src_ref=point_ref,
            dst_ref=points.at[step],
            send_sem=point_send.at[step],
            recv_sem=point_recv.at[step],
            device_id={"sub": (sub_at + step) % subs},
            device_id_type=MESH,
        )

    halo_start(0)
    for step in range(1, subs):
        point_copy(step).start()

    def features(ref, at, xyz, own):
        one, two, three = split3(xyz)
        square = xyz[0:1] * xyz[0:1] + xyz[1:2] * xyz[1:2] + xyz[2:3] * xyz[2:3]
        pieces = [one, one, two, two, one, three] if own else [one, two, one, two, three, one]
        for slot, piece in enumerate(pieces):
            ref[3 * slot : 3 * slot + 3, at] = piece if own else -2.0 * piece
        parts = split3(square)
        for slot in range(3):
            ones = jnp.ones_like(square)
            ref[18 + slot : 19 + slot, at] = parts[slot] if own else ones
            ref[21 + slot : 22 + slot, at] = ones if own else parts[slot]

    inverse_radius = 1.0 / support_radius
    base_xyz = base_ref[:, pl.ds(pl.multiple_of(base_start, LANES), base_own)]
    features(base_feat, slice(None), (base_xyz - 0.5) * inverse_radius, False)

    def build_kernel(step):
        xyz = point_ref[...] if step == 0 else points[step]
        features(cell_feat, slice(None), (xyz - 0.5) * inverse_radius, True)

        def tile(index, carry):
            source = pl.ds(pl.multiple_of(index * TILE, TILE), TILE)
            target = pl.ds(pl.multiple_of(step * cell_count + index * TILE, TILE), TILE)
            mine = cell_feat[:, source].T.astype(jnp.bfloat16)
            for left in range(0, base_own, TILE):
                other = base_feat[:, left : left + TILE].astype(jnp.bfloat16)
                squared = jnp.dot(mine, other, preferred_element_type=jnp.float32)
                squared = jnp.maximum(squared, 1e-20)
                ratio = squared * lax.rsqrt(squared)
                inside = jnp.maximum(1.0 - ratio, 0.0)
                inside = inside * inside
                value = inside * inside * (4.0 * ratio + 1.0)
                hi, lo = split2(value)
                k_hi[target, left : left + TILE] = hi
                k_lo[target, left : left + TILE] = lo
            return carry

        lax.fori_loop(0, cell_count // TILE, tile, 0)

    def relax(sweep):
        stride = ROWS // nodes_here
        for start in range(win.shape[0]):
            for comp in range(5):
                at = start * nodes_here
                win[start, comp] = wide[sweep, comp, at : at + ROWS, :]

        def face_step(face, coupled):
            beside = [[] for _ in range(5)]
            for piece in range(rows // ROWS):
                span = slice(piece * ROWS, (piece + 1) * ROWS)
                rel, lane = rel_ref[face, span, :], lane_ref[face, span, :]
                found = [jnp.zeros((ROWS, LANES), jnp.float32)] * 5
                for chunk in range(2 * blocks + 1):
                    match = rel == chunk
                    for comp in range(5):
                        taken = jnp.take_along_axis(
                            win[chunk + stride * piece, comp], lane, axis=1
                        )
                        found[comp] = jnp.where(match, taken, found[comp])
                for comp in range(5):
                    beside[comp].append(found[comp])
            beside = [jnp.concatenate(part, axis=0) for part in beside]
            coupled = list(coupled)
            for a in range(5):
                for b in range(5):
                    block = off_ref[face, 5 * a + b].astype(jnp.float32)
                    coupled[a] = coupled[a] + block * beside[b]
            return tuple(coupled)

        zero = jnp.zeros((rows, LANES), jnp.float32)
        coupled = lax.fori_loop(0, off_ref.shape[0], face_step, (zero,) * 5)
        if sweep == 0:
            inv_load.wait()
        rest = [rhs_ref[b] - coupled[b] for b in range(5)]
        result = []
        for a in range(5):
            total = inv_ref[5 * a] * rest[0]
            for b in range(1, 5):
                total = total + inv_ref[5 * a + b] * rest[b]
            result.append(total)
        return result

    build_kernel(0)
    halo_wait(0)
    off_load.wait()
    first = relax(0)
    for a in range(5):
        wide[1, a, rows : 2 * rows, :] = first[a]
    halo_start(1)
    for step in range(1, subs):
        point_copy(step).wait_recv()
        build_kernel(step)
    halo_wait(1)
    adjoint = relax(1)
    for a in range(5):
        out_ref[a] = adjoint[a]

    for k in range(3):
        total = adjoint[0] * sens_ref[k].astype(jnp.float32)
        for a in range(1, 5):
            total = total + adjoint[a] * sens_ref[3 * a + k].astype(jnp.float32)
        sens_rows[k] = total
    for k in range(3):
        total = weight_ref[0] * sens_rows[k, pl.ds(0, blocks, stride=nodes_here), :]
        for n in range(1, nodes_here):
            total = total + weight_ref[n] * sens_rows[k, pl.ds(n, blocks, stride=nodes_here), :]
        sens_slots[team, k] = total

    def sens_copy(step):
        return pltpu.make_async_remote_copy(
            src_ref=sens_slots.at[team],
            dst_ref=sens_slots.at[team],
            send_sem=sens_send.at[step],
            recv_sem=sens_recv.at[team],
            device_id=member((team + step) % crew),
            device_id_type=MESH,
        )

    def sens_arrival(step):
        slot = (team + step) % crew
        return pltpu.make_async_remote_copy(
            src_ref=sens_slots.at[slot],
            dst_ref=sens_slots.at[slot],
            send_sem=sens_send.at[step],
            recv_sem=sens_recv.at[slot],
            device_id=member((team + step) % crew),
            device_id_type=MESH,
        )

    for step in range(1, crew):
        sens_copy(step).start()
    sens_mat[...] = jnp.zeros_like(sens_mat)
    for step in range(1, crew):
        sens_arrival(step).wait_recv()
    for step in range(subs):
        whose = (sub_at - step + subs) % subs
        for k in range(3):
            total = sens_slots[whose, k]
            for n in range(1, nodes):
                total = total + sens_slots[n * subs + whose, k]
            hi = total.astype(jnp.bfloat16).astype(jnp.float32)
            lo = total - hi
            for block in range(blocks):
                at = step * cell_count + block * LANES
                sens_mat[k : k + 1, at : at + LANES] = hi[block : block + 1, :]
                sens_mat[ROWS + k : ROWS + k + 1, at : at + LANES] = lo[block : block + 1, :]

    left = sens_mat[...].astype(jnp.bfloat16)
    product = jnp.dot(left, k_hi[...], preferred_element_type=jnp.float32)
    product = product + jnp.dot(left, k_lo[...], preferred_element_type=jnp.float32)
    base_grad = (product[0:ROWS] + product[ROWS:]) * scale
    hi = base_grad.astype(jnp.bfloat16).astype(jnp.float32)
    left = jnp.concatenate([hi, base_grad - hi], axis=0).astype(jnp.bfloat16)
    contract = (((1,), (1,)), ((), ()))
    product = lax.dot_general(left, l_hi[...], contract, preferred_element_type=jnp.float32)
    product = product + lax.dot_general(
        left, l_lo[...], contract, preferred_element_type=jnp.float32
    )
    own = product[0:ROWS] + product[ROWS:]
    for block in range(FFD // LANES):
        grad_slots[me, 3 * block : 3 * block + 3, :] = own[
            0:3, block * LANES : (block + 1) * LANES
        ]

    def grad_copy(step, slot):
        return pltpu.make_async_remote_copy(
            src_ref=grad_slots.at[slot],
            dst_ref=grad_slots.at[slot],
            send_sem=grad_send.at[step],
            recv_sem=grad_recv.at[slot],
            device_id=anyone((me + step) % everyone),
            device_id_type=MESH,
        )

    for step in range(1, everyone):
        grad_copy(step, me).start()
    halo_sent(0)
    halo_sent(1)
    for step in range(1, subs):
        point_copy(step).wait_send()
    for step in range(1, crew):
        sens_copy(step).wait_send()
    for step in range(1, everyone):
        grad_copy(step, (me + step) % everyone).wait_recv()
    total = grad_slots[0]
    for slot in range(1, everyone):
        total = total + grad_slots[slot]
    for block in range(FFD // LANES):
        grad_ref[:, block * LANES : (block + 1) * LANES] = total[3 * block : 3 * block + 3, :]
    for step in range(1, everyone):
        grad_copy(step, me).wait_send()


def to_rows(array):
    array = jnp.moveaxis(array, 0, -2)
    lead, (nodes, cells) = array.shape[:-2], array.shape[-2:]
    array = array.reshape(lead + (nodes, cells // LANES, LANES))
    array = jnp.swapaxes(array, -3, -2)
    return array.reshape(lead + (nodes * cells // LANES, LANES))


def from_rows(array, nodes):
    lead, rows = array.shape[:-2], array.shape[-2]
    array = array.reshape(lead + (rows // nodes, nodes, LANES))
    array = jnp.swapaxes(array, -3, -2).reshape(lead + (nodes, rows // nodes * LANES))
    return jnp.moveaxis(array, -2, 0)


def body(
    adjoint_start,
    adjoint_rhs,
    off_blocks,
    diag_inverse,
    neighbours,
    node_weights,
    sens_blocks,
    cell_points,
    base_points,
    ffd_index,
    ffd_weight,
):
    nodes_here, _, cell_count = adjoint_start.shape
    faces = off_blocks.shape[1]
    cells, subs, nodes = (lax.axis_size(a) for a in ("cells", "sub", "nodes"))
    crew = nodes * subs
    everyone = cells * crew
    blocks = cell_count // LANES
    rows = blocks * nodes_here
    base_own = base_points.shape[1] // crew
    windows = 2 * blocks + 1 + (rows // ROWS - 1) * (ROWS // nodes_here)
    scale = 1.0 / float(cell_count * cells * subs) ** 0.5
    vmem = pl.BlockSpec(memory_space=pltpu.VMEM)
    hbm = pl.BlockSpec(memory_space=pl.ANY)
    f32, bf16 = jnp.float32, jnp.bfloat16
    dma = pltpu.SemaphoreType.DMA
    off_rows, inv_rows = to_rows(off_blocks), to_rows(diag_inverse)
    adjoint, control = pl.pallas_call(
        functools.partial(kernel, scale),
        out_shape=(
            jax.ShapeDtypeStruct((5, rows, LANES), f32),
            jax.ShapeDtypeStruct((3, FFD), f32),
        ),
        in_specs=[pl.BlockSpec(memory_space=pltpu.SMEM)] + [vmem] * 8 + [hbm] * 2,
        out_specs=(vmem, vmem),
        scratch_shapes=[
            pltpu.VMEM(off_rows.shape, bf16),
            pltpu.VMEM(inv_rows.shape, f32),
            pltpu.VMEM((SWEEPS, 5, 3 * rows, LANES), f32),
            pltpu.VMEM((windows, 5, ROWS, LANES), f32),
            pltpu.VMEM((faces, rows, LANES), jnp.int32),
            pltpu.VMEM((faces, rows, LANES), jnp.int32),
            pltpu.VMEM((subs, 3, cell_count), f32),
            pltpu.VMEM((24, cell_count), f32),
            pltpu.VMEM((24, base_own), f32),
            pltpu.VMEM((subs * cell_count, base_own), bf16),
            pltpu.VMEM((subs * cell_count, base_own), bf16),
            pltpu.VMEM((FFD, base_own), bf16),
            pltpu.VMEM((FFD, base_own), bf16),
            pltpu.VMEM((3, rows, LANES), f32),
            pltpu.VMEM((crew, 3, blocks, LANES), f32),
            pltpu.VMEM((2 * ROWS, subs * cell_count), f32),
            pltpu.VMEM((everyone, 3 * FFD // LANES, LANES), f32),
            dma((2,)),
            dma((SWEEPS, 2)),
            dma((SWEEPS, 2)),
            dma((subs,)),
            dma((subs,)),
            dma((crew,)),
            dma((crew,)),
            dma((everyone,)),
            dma((everyone,)),
        ],
        compiler_params=pltpu.CompilerParams(
            collective_id=0, has_side_effects=True, vmem_limit_bytes=60 * 1024 * 1024
        ),
    )(
        node_weights,
        to_rows(adjoint_start),
        to_rows(adjoint_rhs),
        neighbours,
        to_rows(sens_blocks),
        cell_points,
        base_points,
        ffd_index.T,
        ffd_weight.T,
        off_rows,
        inv_rows,
    )
    return from_rows(adjoint, nodes_here), control


def solution(mesh):
    return jax.shard_map(
        body,
        mesh=mesh,
        in_specs=(
            P("nodes", None, ("groups", "cells", "sub")),
            P("nodes", None, ("groups", "cells", "sub")),
            P("nodes", None, None, ("groups", "cells", "sub")),
            P("nodes", None, ("groups", "cells", "sub")),
            P(None, ("cells", "sub")),
            P("nodes"),
            P("nodes", None, ("groups", "cells", "sub")),
            P(None, ("cells", "sub")),
            P(),
            P(),
            P(),
        ),
        out_specs=(P("nodes", None, ("groups", "cells", "sub")), P("groups", None)),
        check_vma=False,
    )
```

time: 311 us -> 28.2 us (0.09)
  local copies, waits for them, and re-layouts: 105 us -> 2.01 us
  other arithmetic: 65 us -> 0 us
  waiting for transfers between devices: 63.1 us -> 0 us
  blocking collectives: 38.8 us -> 0 us
  Pallas kernels: 0 us -> 25.4 us
  between operations: 14.8 us -> 0.65 us
  matrix products: 11.9 us -> 0 us
  starting transfers between devices: 10.4 us -> 0 us
    gather x12 -> x0, local copies, waits for them, and re-layouts: 79.7 us -> none  [relax(): widened[:, :, local_index[face_slot]]]
    unnamed x2 -> x0, waiting for transfers between devices: 63.1 us -> none
    select_n x14 -> x0, other arithmetic: 50.5 us -> none  [the longest x12 49.7 us: relax(): jnp.where(present[face_slot][None, None, :], widened[:, :, local_index[fa...]
    psum x2 -> x0, blocking collectives: 38.8 us -> none  [the longest x1 30.6 us: body(): control_grad = lax.psum(own_grad, ('cells', 'nodes', 'sub'))]
    pallas_call x0 -> x1, Pallas kernels: none -> 25.4 us  [body(): pl.pallas_call(functools.partial(kernel, scale), out_shape=(jax.ShapeDtyp...]
    dot_general x9 -> x0, matrix products: 11.9 us -> none  [the longest x8 11.6 us: kernel_sum(): jnp.dot(sensitivity, kernel, precision=lax.Precision.HIGHEST, preferred_e...]
    reduce_sum x17 -> x0, other arithmetic: 10.6 us -> none  [the longest x12 7.63 us: relax(): coupled = coupled + jnp.sum(coupling * beside[:, None], axis=2)]
    ppermute x4 -> x0, starting transfers between devices: 10.4 us -> none  [the longest x2 7.65 us: with_halo(): before = lax.ppermute(last, axis, up)]
  transfers between devices with their start and end apart: 5 -> 0, of which waited for: 1 -> 0; matrix products, arithmetic and copies ran while one was open for 4% -> 0% of each run, Pallas kernels for 0% -> 0%
where the time goes in v1:
time: 28.2 us; the launch traced here: 28 us
  Pallas kernels  25.4 us (90%)
  local copies, waits for them, and re-layouts  2.01 us (7%)
  between operations  0.65 us (2%)
    pallas_call x1, Pallas kernels, body(): pl.pallas_call(functools.partial(kernel, scale), out_shape=(jax.ShapeDtyp...  25.4 us
    unnamed x4, local copies, waits for them, and re-layouts  2.01 us

profile of v1, /device:TPU:0, one launch (start us, length us, event | category | flops | bytes accessed | tf_op | source)
XLA Modules:
  0.0 28.0 jit_solution(18346973096689648884)
XLA Ops:
  0.6 25.4 %shard_map.122 = (f32[5,16,128]{2,1,0:T(8,128)}, f32[3,512]{1,0:T(4,128)}) custom-call(f32[2]{0:T(128)} %weight_ref.1, f32[5,16,128]{2,1,0:T(8,128)} %bitcast.49, f32[5,16,128]{2,1,0:T(8,128)} %bitcast.50, s32[6,1024]{1,0:T(8,128)} %nb_ref.1, bf16[15,16,128]{2,1,0:T(8,128)(2,1)} %bitcast.48, f32[3,1024]{1,0:T(4,128)} %point_ref.1, f32[3,4096]{1,0:T(4,128)} %base_ref.1, ...), custom_call_target="tpu_custom_call" | custom-call | tf_op jit(solution)/shard_map/pallas_call | solution.py:432
  26.0 0.0 copy-start
  26.0 1.4 %copy.20 = f32[2,5,1024]{2,0,1:T(2,128)} copy(f32[2,5,1024]{2,0,1:T(2,128)} %bitcast.51) | data formatting | bytes 81920
  27.4 0.0 copy-done
  27.4 0.6 %copy.21 = f32[3,512]{1,0:T(4,128)} copy(f32[3,512]{1,0:T(4,128)S(1)} %copy-done) | data formatting | bytes 12288
Async XLA Ops:
  26.0 1.4 %copy-start = (f32[3,512]{1,0:T(4,128)S(1)}, f32[3,512]{1,0:T(4,128)}, u32[]{:S(2)}) copy-start(f32[3,512]{1,0:T(4,128)} %get-tuple-element.9) | copy-start | bytes 18436

commit v2 on v1

--- a/solution.py
+++ b/solution.py
@@ -31,20 +31,27 @@
 def kernel(
     scale,
     weight_ref,
-    adj_ref,
+    adj_hbm,
+    point_hbm,
+    nb_hbm,
+    base_hbm,
+    off_hbm,
+    rhs_hbm,
+    inv_hbm,
+    sens_hbm,
+    ffd_index_hbm,
+    ffd_weight_hbm,
+    out_ref,
+    grad_ref,
+    point_ref,
+    nb_ref,
+    base_ref,
+    off_ref,
     rhs_ref,
-    nb_ref,
+    inv_ref,
     sens_ref,
-    point_ref,
-    base_ref,
     ffd_index_ref,
     ffd_weight_ref,
-    off_hbm,
-    inv_hbm,
-    out_ref,
-    grad_ref,
-    off_ref,
-    inv_ref,
     wide,
     win,
     rel_ref,
@@ -69,6 +76,7 @@
     sens_recv,
     grad_send,
     grad_recv,
+    known,
 ):
     cells, subs, nodes = (lax.axis_size(a) for a in ("cells", "sub", "nodes"))
     cell_at, sub_at, node_at = (lax.axis_index(a) for a in ("cells", "sub", "nodes"))
@@ -76,7 +84,7 @@
     team, crew = node_at * subs + sub_at, nodes * subs
     me, everyone = cell_at * crew + team, cells * crew
     nodes_here = weight_ref.shape[0]
-    rows = adj_ref.shape[1]
+    rows = adj_hbm.shape[1]
     blocks = rows // nodes_here
     cell_count = blocks * LANES
     base_own = base_feat.shape[1]
@@ -87,18 +95,68 @@
     def anyone(index):
         return dict(member(index % crew), cells=index // crew)
 
+    lower, upper = cell_at > 0, cell_at < cells - 1
+    below, above = cell_at - 1, cell_at + 1
+
     barrier = pltpu.get_barrier_semaphore()
-    for step in range(1, everyone):
-        pl.semaphore_signal(
-            barrier, inc=1, device_id=anyone((me + step) % everyone), device_id_type=MESH
-        )
-    off_load = pltpu.make_async_copy(off_hbm, off_ref, load_sem.at[0])
-    inv_load = pltpu.make_async_copy(inv_hbm, inv_ref, load_sem.at[1])
-    off_load.start()
-    inv_load.start()
-
-    wide[0, :, rows : 2 * rows, :] = adj_ref[...]
-
+
+    def greet(device):
+        pl.semaphore_signal(barrier, inc=1, device_id=device, device_id_type=MESH)
+
+    greeted = crew - 1
+    for step in range(1, crew):
+        greet(member((team + step) % crew))
+    greetings = [(lower, {"cells": below}), (upper, {"cells": above})]
+    if subs > 1:
+        first, last = sub_at == 0, sub_at == subs - 1
+        greetings.append((jnp.logical_and(lower, first), {"cells": below, "sub": subs - 1}))
+        greetings.append((jnp.logical_and(upper, last), {"cells": above, "sub": 0}))
+    for exists, device in greetings:
+        pl.when(exists)(functools.partial(greet, device))
+        greeted = greeted + exists.astype(jnp.int32)
+
+    base_start = pl.multiple_of(team * base_own, LANES)
+    share = pl.ds(base_start, base_own)
+    sources = (
+        (adj_hbm, wide.at[0, :, pl.ds(rows, rows), :]),
+        (point_hbm, point_ref),
+        (nb_hbm, nb_ref),
+        (base_hbm.at[:, share], base_ref),
+        (off_hbm, off_ref),
+        (rhs_hbm, rhs_ref),
+        (inv_hbm, inv_ref),
+        (sens_hbm, sens_ref),
+        (ffd_index_hbm.at[:, share], ffd_index_ref),
+        (ffd_weight_hbm.at[:, share], ffd_weight_ref),
+    )
+    loads = [
+        pltpu.make_async_copy(source, target, load_sem.at[slot])
+        for slot, (source, target) in enumerate(sources)
+    ]
+    for load in loads:
+        load.start()
+    (adj_load, point_load, nb_load, base_load, off_load, rhs_load, inv_load, sens_load) = loads[:8]
+
+    def tell(stage):
+        for side, (exists, other) in enumerate(((upper, above), (lower, below))):
+
+            @pl.when(exists)
+            def _():
+                pl.semaphore_signal(
+                    known.at[stage, side],
+                    inc=1,
+                    device_id={"cells": other},
+                    device_id_type=MESH,
+                )
+
+    def hear(stage):
+        for side, exists in enumerate((lower, upper)):
+
+            @pl.when(exists)
+            def _():
+                pl.semaphore_wait(known.at[stage, side], 1)
+
+    nb_load.wait()
     first_cell = here * cell_count
     for face in range(nb_ref.shape[0]):
         for block in range(blocks):
@@ -109,13 +167,10 @@
             rel_ref[face, span, :] = jnp.broadcast_to(chunk, (nodes_here, LANES))
             lane_ref[face, span, :] = jnp.broadcast_to(local & (LANES - 1), (nodes_here, LANES))
 
-    base_start = team * base_own
-
     def build_lattice(step, carry):
-        source = pl.ds(pl.multiple_of(base_start + step * LANES, LANES), LANES)
         target = pl.ds(pl.multiple_of(step * LANES, LANES), LANES)
-        index = ffd_index_ref[:, source]
-        weight = ffd_weight_ref[:, source]
+        index = ffd_index_ref[:, target]
+        weight = ffd_weight_ref[:, target]
         group = 64
         row = lax.broadcasted_iota(jnp.int32, (group, LANES), 0)
         for top in range(0, FFD, group):
@@ -128,7 +183,6 @@
             l_lo[top : top + group, target] = lo
         return carry
 
-    lax.fori_loop(0, base_own // LANES, build_lattice, 0)
 
     @pl.when(here == 0)
     def _():
@@ -138,7 +192,9 @@
     def _():
         wide[:, :, 2 * rows : 3 * rows, :] = jnp.zeros((SWEEPS, 5, rows, LANES), jnp.float32)
 
-    pl.semaphore_wait(barrier, everyone - 1)
+    adj_load.wait()
+    point_load.wait()
+    pl.semaphore_wait(barrier, greeted)
 
     def halo(sweep, side):
         other = here + 1 if side == 0 else here - 1
@@ -192,6 +248,8 @@
     halo_start(0)
     for step in range(1, subs):
         point_copy(step).start()
+    tell(0)
+    base_load.wait()
 
     def features(ref, at, xyz, own):
         one, two, three = split3(xyz)
@@ -206,8 +264,7 @@
             ref[21 + slot : 22 + slot, at] = ones if own else parts[slot]
 
     inverse_radius = 1.0 / support_radius
-    base_xyz = base_ref[:, pl.ds(pl.multiple_of(base_start, LANES), base_own)]
-    features(base_feat, slice(None), (base_xyz - 0.5) * inverse_radius, False)
+    features(base_feat, slice(None), (base_ref[...] - 0.5) * inverse_radius, False)
 
     def build_kernel(step):
         xyz = point_ref[...] if step == 0 else points[step]
@@ -265,6 +322,7 @@
         zero = jnp.zeros((rows, LANES), jnp.float32)
         coupled = lax.fori_loop(0, off_ref.shape[0], face_step, (zero,) * 5)
         if sweep == 0:
+            rhs_load.wait()
             inv_load.wait()
         rest = [rhs_ref[b] - coupled[b] for b in range(5)]
         result = []
@@ -282,6 +340,9 @@
     for a in range(5):
         wide[1, a, rows : 2 * rows, :] = first[a]
     halo_start(1)
+    if cells > 2:
+        hear(0)
+        tell(1)
     for step in range(1, subs):
         point_copy(step).wait_recv()
         build_kernel(step)
@@ -290,6 +351,7 @@
     for a in range(5):
         out_ref[a] = adjoint[a]
 
+    sens_load.wait()
     for k in range(3):
         total = adjoint[0] * sens_ref[k].astype(jnp.float32)
         for a in range(1, 5):
@@ -324,7 +386,13 @@
 
     for step in range(1, crew):
         sens_copy(step).start()
+    for stage in range(2, cells - 1):
+        hear(stage - 1)
+        tell(stage)
     sens_mat[...] = jnp.zeros_like(sens_mat)
+    loads[8].wait()
+    loads[9].wait()
+    lax.fori_loop(0, base_own // LANES, build_lattice, 0)
     for step in range(1, crew):
         sens_arrival(step).wait_recv()
     for step in range(subs):
@@ -367,6 +435,8 @@
             device_id_type=MESH,
         )
 
+    if cells > 1:
+        hear(cells - 2)
     for step in range(1, everyone):
         grad_copy(step, me).start()
     halo_sent(0)
@@ -384,6 +454,11 @@
         grad_ref[:, block * LANES : (block + 1) * LANES] = total[3 * block : 3 * block + 3, :]
     for step in range(1, everyone):
         grad_copy(step, me).wait_send()
+
+
+def finish(adjoint_in, control_in, adjoint_out, control_out):
+    adjoint_out[...] = adjoint_in[...]
+    control_out[...] = control_in[...]
 
 
 def to_rows(array):
@@ -425,21 +500,29 @@
     windows = 2 * blocks + 1 + (rows // ROWS - 1) * (ROWS // nodes_here)
     scale = 1.0 / float(cell_count * cells * subs) ** 0.5
     vmem = pl.BlockSpec(memory_space=pltpu.VMEM)
-    hbm = pl.BlockSpec(memory_space=pl.ANY)
+    hbm = pl.BlockSpec(memory_space=pltpu.HBM)
     f32, bf16 = jnp.float32, jnp.bfloat16
     dma = pltpu.SemaphoreType.DMA
     off_rows, inv_rows = to_rows(off_blocks), to_rows(diag_inverse)
+    sens_cells = to_rows(sens_blocks)
     adjoint, control = pl.pallas_call(
         functools.partial(kernel, scale),
         out_shape=(
             jax.ShapeDtypeStruct((5, rows, LANES), f32),
             jax.ShapeDtypeStruct((3, FFD), f32),
         ),
-        in_specs=[pl.BlockSpec(memory_space=pltpu.SMEM)] + [vmem] * 8 + [hbm] * 2,
+        in_specs=[pl.BlockSpec(memory_space=pltpu.SMEM)] + [hbm] * 10,
         out_specs=(vmem, vmem),
         scratch_shapes=[
+            pltpu.VMEM(cell_points.shape, f32),
+            pltpu.VMEM(neighbours.shape, jnp.int32),
+            pltpu.VMEM((3, base_own), f32),
             pltpu.VMEM(off_rows.shape, bf16),
+            pltpu.VMEM((5, rows, LANES), f32),
             pltpu.VMEM(inv_rows.shape, f32),
+            pltpu.VMEM(sens_cells.shape, bf16),
+            pltpu.VMEM((ffd_index.shape[1], base_own), jnp.int32),
+            pltpu.VMEM((ffd_index.shape[1], base_own), f32),
             pltpu.VMEM((SWEEPS, 5, 3 * rows, LANES), f32),
             pltpu.VMEM((windows, 5, ROWS, LANES), f32),
             pltpu.VMEM((faces, rows, LANES), jnp.int32),
@@ -455,7 +538,7 @@
             pltpu.VMEM((crew, 3, blocks, LANES), f32),
             pltpu.VMEM((2 * ROWS, subs * cell_count), f32),
             pltpu.VMEM((everyone, 3 * FFD // LANES, LANES), f32),
-            dma((2,)),
+            dma((10,)),
             dma((SWEEPS, 2)),
             dma((SWEEPS, 2)),
             dma((subs,)),
@@ -464,23 +547,36 @@
             dma((crew,)),
             dma((everyone,)),
             dma((everyone,)),
+            pltpu.SemaphoreType.REGULAR((max(cells - 1, 1), 2)),
         ],
         compiler_params=pltpu.CompilerParams(
-            collective_id=0, has_side_effects=True, vmem_limit_bytes=60 * 1024 * 1024
+            collective_id=0, has_side_effects=True, vmem_limit_bytes=16 * 1024 * 1024
         ),
     )(
         node_weights,
-        to_rows(adjoint_start),
-        to_rows(adjoint_rhs),
-        neighbours,
-        to_rows(sens_blocks),
-        cell_points,
-        base_points,
-        ffd_index.T,
-        ffd_weight.T,
-        off_rows,
-        inv_rows,
+        *(pltpu.with_memory_space_constraint(array, pltpu.HBM) for array in (
+            to_rows(adjoint_start),
+            cell_points,
+            neighbours,
+            base_points,
+            off_rows,
+            to_rows(adjoint_rhs),
+            inv_rows,
+            sens_cells,
+            ffd_index.T,
+            ffd_weight.T,
+        ))
     )
+    adjoint, control = pl.pallas_call(
+        finish,
+        out_shape=(
+            jax.ShapeDtypeStruct((5, rows, LANES), f32),
+            jax.ShapeDtypeStruct((3, FFD), f32),
+        ),
+        in_specs=[vmem] * 2,
+        out_specs=(vmem, vmem),
+        compiler_params=pltpu.CompilerParams(vmem_limit_bytes=1024 * 1024),
+    )(adjoint, control)
     return from_rows(adjoint, nodes_here), control
 
 

time: 28.2 us -> 25.4 us (0.901)
  Pallas kernels: 25.4 us -> 24 us
  local copies, waits for them, and re-layouts: 2.01 us -> 0.65 us
    pallas_call x1, Pallas kernels: 25.4 us -> 23.3 us  [body(): pl.pallas_call(functools.partial(kernel, scale), out_shape=(jax.ShapeDtyp...]
    unnamed x4 -> x2, local copies, waits for them, and re-layouts: 2.01 us -> 0.65 us
    pallas_call x0 -> x1, Pallas kernels: none -> 0.62 us  [body(): pl.pallas_call(finish, out_shape=(jax.ShapeDtypeStruct((5, rows, LANES),...]
where the time goes in v2:
time: 25.4 us; the launch traced here: 25.3 us
  Pallas kernels  24 us (94%)
  local copies, waits for them, and re-layouts  0.65 us (3%)
  between operations  0.65 us (3%)
    pallas_call x1, Pallas kernels, body(): pl.pallas_call(functools.partial(kernel, scale), out_shape=(jax.ShapeDtyp...  23.3 us
    unnamed x2, local copies, waits for them, and re-layouts  0.65 us
    pallas_call x1, Pallas kernels, body(): pl.pallas_call(finish, out_shape=(jax.ShapeDtypeStruct((5, rows, LANES),...  0.62 us

profile of v2, /device:TPU:0, one launch (start us, length us, event | category | flops | bytes accessed | tf_op | source)
XLA Modules:
  0.0 25.3 jit_solution(16172453545033344468)
XLA Ops:
  0.6 0.0 copy-start
  0.6 0.6 %copy-done = f32[2]{0:T(128)S(1)} copy-done((f32[2]{0:T(128)S(1)}, f32[2]{0:T(128)}, u32[]{:S(2)}) %copy-start) | copy-done | bytes 32
  1.3 23.3 %shard_map.122 = (f32[5,16,128]{2,1,0:T(8,128)S(1)}, f32[3,512]{1,0:T(4,128)S(1)}) custom-call(f32[2]{0:T(128)S(1)} %copy-done, f32[5,16,128]{2,1,0:T(8,128)} %bitcast.49, f32[3,1024]{1,0:T(4,128)} %point_hbm.1, s32[6,1024]{1,0:T(8,128)} %nb_hbm.1, f32[3,4096]{1,0:T(4,128)} %base_hbm.1, bf16[6,25,16,128]{3,2,1,0:T(8,128)(2,1)} %bitcast.44, ...), custom_call_target="tpu_custom_call" | custom-call | tf_op jit(solution)/shard_map/pallas_call | solution.py:508
  24.6 0.6 %shard_map.123 = (f32[5,16,128]{2,1,0:T(8,128)}, f32[3,512]{1,0:T(4,128)}) custom-call(f32[5,16,128]{2,1,0:T(8,128)S(1)} %get-tuple-element.6.adjoint_in, f32[3,512]{1,0:T(4,128)S(1)} %get-tuple-element.7.control_in), custom_call_target="tpu_custom_call" | custom-call | tf_op jit(solution)/shard_map/pallas_call | solution.py:570
Async XLA Ops:
  0.6 0.7 %copy-start = (f32[2]{0:T(128)S(1)}, f32[2]{0:T(128)}, u32[]{:S(2)}) copy-start(f32[2]{0:T(128)} %weight_ref.1) | copy-start | bytes 28
